TPU v7x, 32 devices: a whole 2x2x4 slice. The times are simulated.
32 devices in a mesh: dp: 8 (over y, x, core), vocab: 4 (over z).
Axes of the slice: x: 2, y: 2, z: 4, core: 2. Of those that a mesh axis runs over, the one named last changes fastest.
Arguments:
- hidden: bfloat16 [3840, 4096], P('dp', 'vocab'), may hold values from -8 to 8
- head: bfloat16 [4096, 2048], P(None, 'vocab'), may hold values from -3 to 3
- shortlist: int32 [16, 8], P('dp', 'vocab'), may hold values from 0 to 1, as said below
- tokens: int32 [3840], P('dp'), may hold values from 0 to 2047, as said below
- risk: int32 [16, 12], P('dp'), may hold values from 0 to 100
Outputs:
- hidden_grad: bfloat16 [3840, 4096], P(('dp', 'vocab'))
- head_grad: float32 [4096, 2048], P('dp', 'vocab')
- expected: float32 [16], P('dp')
Inputs may be any that keep to these rules, and one draw needn't show every extreme that they name: Every sentence's shortlist holds at least one block. `tokens`: each token's word lies in a block that its sentence's shortlist holds.
All inputs are finite; a program needn't handle non-finite values.
Results may differ from a plain program's by a relative error of at most 0.013.
Values may be sent and summed in bfloat16 or wider, within the bound.
No kernel may reach another device: no remote copies, remote signals or barrier semaphores. Data moves between devices by JAX's collectives and lax.ppermute only.
A program may use at most 64 MiB of HBM per device.

v0:
```python
import jax
import jax.numpy as jnp
from jax import lax
from jax.sharding import PartitionSpec as P

masked_value = -1e30
loss_scale = 2048.0


def add_pieces(received):
    return jnp.sum(received.astype(jnp.float32), axis=0)


def body(hidden, head, shortlist, tokens, risk):
    features = lax.all_gather(hidden, "vocab", axis=1, tiled=True)
    row_count = features.shape[0]
    sent_count = shortlist.shape[0]
    cand_count = risk.shape[1]
    per_sentence = row_count // sent_count
    seq_length = per_sentence // cand_count
    col_count = head.shape[1]
    block_width = col_count // shortlist.shape[1]
    col_offset = lax.axis_index("vocab") * col_count
    expanded = jnp.repeat(shortlist, block_width, axis=1) == 1
    allowed = jnp.broadcast_to(expanded[:, None, :], (sent_count, per_sentence, col_count)).reshape(
        row_count, col_count
    )
    target_hit = (tokens - col_offset)[:, None] == jnp.arange(col_count, dtype=jnp.int32)[None, :]
    logits = jnp.dot(features, head, preferred_element_type=jnp.float32)
    masked = jnp.where(allowed, logits, masked_value)
    row_peak = jnp.max(masked, axis=1)
    row_total = jnp.sum(jnp.where(allowed, jnp.exp(masked - row_peak[:, None]), 0.0), axis=1)
    chosen = jnp.sum(jnp.where(target_hit, logits, 0.0), axis=1)
    global_peak = lax.pmax(row_peak, "vocab")
    global_total, target_logit = lax.psum(
        (row_total * jnp.exp(row_peak - global_peak), chosen), "vocab"
    )
    logprob = target_logit - global_peak - jnp.log(global_total)
    scores = jnp.mean(logprob.reshape(sent_count, cand_count, seq_length), axis=2)
    raised = jnp.exp(scores)
    weights = raised / jnp.sum(raised, axis=1, keepdims=True)
    cost_value = risk.astype(jnp.float32) / 100.0
    expected = jnp.sum(weights * cost_value, axis=1)
    cand_coeff = loss_scale * weights * (cost_value - expected[:, None]) / seq_length
    row_coeff = jnp.broadcast_to(
        cand_coeff[:, :, None], (sent_count, cand_count, seq_length)
    ).reshape(row_count)
    row_prob = (
        jnp.where(allowed, jnp.exp(masked - global_peak[:, None]), 0.0) / global_total[:, None]
    )
    grad_logits = (row_coeff[:, None] * (target_hit.astype(jnp.float32) - row_prob)).astype(
        jnp.bfloat16
    )
    model_width = features.shape[1]
    vocab_count = lax.axis_size("vocab")
    share_rows = row_count // vocab_count
    piece = grad_logits
    partial_value = (
        lax.dot_general(piece, head, (((1,), (1,)), ((), ())), preferred_element_type=jnp.float32)
        .astype(jnp.bfloat16)
        .reshape(vocab_count, share_rows, model_width)
    )
    summed = add_pieces(
        lax.all_to_all(partial_value, "vocab", split_axis=0, concat_axis=0, tiled=True)
    )
    hidden_grad = summed.astype(jnp.bfloat16)
    piece = features
    head_grad = lax.psum_scatter(
        lax.dot_general(
            piece, grad_logits, (((0,), (0,)), ((), ())), preferred_element_type=jnp.float32
        ).astype(jnp.bfloat16),
        "dp",
        scatter_dimension=0,
        tiled=True,
    ).astype(jnp.float32)
    return (hidden_grad, head_grad, expected)


def solution(mesh):
    return jax.shard_map(
        body,
        mesh=mesh,
        in_specs=(P("dp", "vocab"), P(None, "vocab"), P("dp", "vocab"), P("dp"), P("dp", None)),
        out_specs=(P(("dp", "vocab"), None), P("dp", "vocab"), P("dp")),
        check_vma=False,
    )
```

profile of v0, /device:TPU:0, one launch (start us, length us, event | category | flops | bytes accessed | tf_op | source)
XLA Modules:
  0.0 226.2 jit_solution(11814001783352340421)
XLA Ops:
  7.2 0.7 all-gather.2.cloned.1.call-update
  7.9 0.0 reduce-scatter.2.cloned.1.call-start
  7.9 0.7 broadcast_compare_fusion
  8.6 0.1 broadcast_bitcast_fusion
  8.7 0.7 broadcast_subtract_fusion
  9.4 79.3 %all-gather.2.cloned.1.call-done = bf16[480,4096]{1,0:T(8,128)(2,1)} async-done(((bf16[480,1024]{1,0:T(8,128)(2,1)}), bf16[480,4096]{1,0:T(8,128)(2,1)}) %all-gather.2.cloned.1.call-update) | async-done | bytes 3932176 | tf_op jit(solution)/shard_map/all_gather | solution.py:15
  88.7 0.1 broadcast_in_dim.17
  88.8 5.7 %fusion.1 = (f32[480]{0:T(512)S(1)}, f32[480,512]{1,0:T(8,128)S(1)}) fusion(pred[480,512]{1,0:T(8,128)(4,1)S(1)} %bitcast.15, bf16[480,4096]{1,0:T(8,128)(2,1)} %all-gather.2.cloned.1.call-done, bf16[4096,512]{1,0:T(8,128)(2,1)} %param.6), kind=kOutput, calls=%fused_computation.8 | convolution fusion | flops 2013756928 | bytes 9357184 | tf_op jit(solution)/shard_map/dot_general | solution.py:29
  94.5 9.0 %pmax.7 = f32[480]{0:T(512)S(1)} all-reduce(f32[480]{0:T(512)S(1)} %get-tuple-element.15), channel_id=1, replica_groups=mesh['dp'=8,'vocab'=4] {'vocab'}, use_global_device_ids=true, to_apply=%region_3.4 | all-reduce | flops 480 | bytes 3840 | tf_op jit(solution)/shard_map/pmax | solution.py:34
  103.5 0.7 select_reduce_fusion.1
  104.1 9.8 %all-reduce = (f32[480]{0:T(512)S(1)}, f32[480]{0:T(512)S(1)}) all-reduce(f32[480]{0:T(512)S(1)} %exponential_multiply_fusion, f32[480]{0:T(512)S(1)} %get-tuple-element.9), channel_id=1, replica_groups=mesh['dp'=8,'vocab'=4] {'vocab'}, use_global_device_ids=true, to_apply=%region_5.6 | all-reduce | flops 960 | bytes 7680 | tf_op jit(solution)/shard_map/psum | solution.py:35
  113.9 0.1 reshape.32
  114.0 0.1 reduce_sum.59
  114.1 0.1 fusion.3
  114.2 0.2 multiply_reduce_fusion
  114.4 0.1 multiply_multiply_fusion
  114.5 0.1 broadcast_in_dim.35
  114.6 0.1 mul.30
  114.7 0.4 multiply_convert_fusion
  115.1 6.4 %fusion = bf16[4096,512]{0,1:T(8,128)(2,1)} fusion(bf16[480,512]{1,0:T(8,128)(2,1)S(1)} %multiply_convert_fusion, bf16[480,4096]{1,0:T(8,128)(2,1)} %all-gather.2.cloned.1.call-done), kind=kOutput, calls=%fused_computation.2 | convolution fusion | flops 2015363072 | bytes 8617984 | tf_op jit(solution)/shard_map/dot_general | solution.py:69
  121.6 4.5 %convolution_convert_fusion.1 = bf16[480,4096]{1,0:T(8,128)(2,1)S(1)} fusion(bf16[480,512]{1,0:T(8,128)(2,1)S(1)} %multiply_convert_fusion, bf16[4096,512]{1,0:T(8,128)(2,1)} %param.6), kind=kOutput, calls=%fused_computation.1 | convolution fusion | flops 2015232000 | bytes 8617984 | tf_op jit(solution)/shard_map/dot_general | solution.py:59
  126.1 87.0 %all_to_all.5 = bf16[4,120,4096]{2,1,0:T(8,128)(2,1)} all-to-all(bf16[4,120,4096]{2,1,0:T(8,128)(2,1)S(1)} %bitcast.14), channel_id=1, replica_groups=mesh['dp'=8,'vocab'=4] {'vocab'}, dimensions={0} | all-to-all | bytes 7864320 | tf_op jit(solution)/shard_map/all_to_all | solution.py:64
  213.1 4.0 %reduce_sum.62 = bf16[120,4096]{1,0:T(8,128)(2,1)} reduce(bf16[4,120,4096]{2,1,0:T(8,128)(2,1)} %all_to_all.5, bf16[]{:T(256)} %constant.24.clone.1), dimensions={0}, to_apply=%region_9.10 | reduce | flops 1474560 | bytes 4915202 | tf_op jit(solution)/shard_map/reduce_sum | solution.py:11
  217.2 2.2 copy.9
  (10 shorter events, 0.1 us)
Async XLA Ops:
  7.2 81.5 %all-gather.2.cloned.1.call-start = ((), (), s32[]{:S(2)}) async-start(), calls=%async_computation.2 | async-start | bytes 4915200 | tf_op jit(solution)/shard_map/all_gather | solution.py:15
  7.9 209.3 %reduce-scatter.2.cloned.1.call-start = ((), (), s32[]{:S(2)}) async-start(), calls=%async_computation.3 | async-start | bytes 4718592 | tf_op jit(solution)/shard_map/reduce_scatter | solution.py:68
  88.8 25.4 %copy-start = (s32[2,12]{1,0:T(2,128)S(1)}, s32[2,12]{1,0:T(2,128)}, u32[]{:S(2)}) copy-start(s32[2,12]{1,0:T(2,128)} %param.9) | copy-start | bytes 292
  114.4 7.1 %copy-start.1 = (f32[2]{0:T(128)}, f32[2]{0:T(128)S(1)}, u32[]{:S(2)}) copy-start(f32[2]{0:T(128)S(1)} %get-tuple-element.13) | copy-start | bytes 28
Sparse Core Ops, SparseCore 0:
  9.5 79.1 all-gather.1
  121.7 49.4 reduce-scatter.1
where the time goes:
time: 227 us; the launch traced here: 226 us
  blocking collectives  106 us (47%)
  waiting for transfers between devices  80 us (35%)
  matrix products  16.6 us (7%)
  between operations  14.1 us (6%)
  other arithmetic  6.99 us (3%)
  local copies, waits for them, and re-layouts  2.66 us (1%)
    all_to_all x1, blocking collectives, body(): lax.all_to_all(partial_value, 'vocab', split_axis=0, concat_axis=0, tiled...  87 us
    all_gather x1, waiting for transfers between devices, body(): features = lax.all_gather(hidden, 'vocab', axis=1, tiled=True)  79.3 us
    psum x1, blocking collectives, body(): lax.psum((row_total * jnp.exp(row_peak - global_peak), chosen), 'vocab')  9.76 us
    pmax x1, blocking collectives, body(): global_peak = lax.pmax(row_peak, 'vocab')  8.99 us
    dot_general x1, matrix products, body(): lax.dot_general(piece, grad_logits, (((0,), (0,)), ((), ())), preferred_e...  6.43 us
    dot_general x1, matrix products, body(): logits = jnp.dot(features, head, preferred_element_type=jnp.float32)  5.67 us
  transfers between devices with their start and end apart: 2, of which 1 were waited for; matrix products, arithmetic and copies ran while one was open for 4% of the time, Pallas kernels for 0%

commit v1 on v0

v1 whole, which is shorter than its diff:
```python
import functools

import jax
import jax.numpy as jnp
from jax import lax
from jax.experimental import pallas as pl
from jax.experimental.pallas import tpu as pltpu
from jax.sharding import PartitionSpec as P


masked_value = -1e30
loss_scale = 2048.0
kernel_vmem = 12 << 20


def add_pieces(received):
    return jnp.sum(received.astype(jnp.float32), axis=0)


def swap_dp(value, bit):
    count = lax.axis_size("dp")
    return lax.ppermute(value, "dp", [(i, i ^ bit) for i in range(count)])


def shift_half(value):
    count = lax.axis_size("vocab")
    return lax.ppermute(value, "vocab", [(i, (i + count // 2) % count) for i in range(count)])


def shift_within(value, step):
    count = lax.axis_size("vocab")
    group = count // 2
    pairs = [(i, i // group * group + (i % group + step) % group) for i in range(count)]
    return lax.ppermute(value, "vocab", pairs)


def after(value, *others):
    return lax.optimization_barrier((value,) + others)[0]


def dp_bits():
    count = lax.axis_size("dp")
    return [1 << b for b in range(count.bit_length() - 1)]


def plain(hidden, head, shortlist, tokens, risk):
    features = lax.all_gather(hidden, "vocab", axis=1, tiled=True)
    row_count = features.shape[0]
    sent_count = shortlist.shape[0]
    cand_count = risk.shape[1]
    per_sentence = row_count // sent_count
    seq_length = per_sentence // cand_count
    col_count = head.shape[1]
    block_width = col_count // shortlist.shape[1]
    col_offset = lax.axis_index("vocab") * col_count
    expanded = jnp.repeat(shortlist, block_width, axis=1) == 1
    allowed = jnp.broadcast_to(expanded[:, None, :], (sent_count, per_sentence, col_count)).reshape(
        row_count, col_count
    )
    target_hit = (tokens - col_offset)[:, None] == jnp.arange(col_count, dtype=jnp.int32)[None, :]
    logits = jnp.dot(features, head, preferred_element_type=jnp.float32)
    masked = jnp.where(allowed, logits, masked_value)
    row_peak = jnp.max(masked, axis=1)
    row_total = jnp.sum(jnp.where(allowed, jnp.exp(masked - row_peak[:, None]), 0.0), axis=1)
    chosen = jnp.sum(jnp.where(target_hit, logits, 0.0), axis=1)
    global_peak = lax.pmax(row_peak, "vocab")
    global_total, target_logit = lax.psum(
        (row_total * jnp.exp(row_peak - global_peak), chosen), "vocab"
    )
    logprob = target_logit - global_peak - jnp.log(global_total)
    expected, cand_coeff = candidate_terms(logprob, risk, seq_length)
    row_coeff = jnp.broadcast_to(
        cand_coeff[:, :, None], (sent_count, cand_count, seq_length)
    ).reshape(row_count)
    row_prob = (
        jnp.where(allowed, jnp.exp(masked - global_peak[:, None]), 0.0) / global_total[:, None]
    )
    grad_logits = (row_coeff[:, None] * (target_hit.astype(jnp.float32) - row_prob)).astype(
        jnp.bfloat16
    )
    model_width = features.shape[1]
    vocab_count = lax.axis_size("vocab")
    share_rows = row_count // vocab_count
    partial_value = (
        lax.dot_general(
            grad_logits, head, (((1,), (1,)), ((), ())), preferred_element_type=jnp.float32
        )
        .astype(jnp.bfloat16)
        .reshape(vocab_count, share_rows, model_width)
    )
    summed = add_pieces(
        lax.all_to_all(partial_value, "vocab", split_axis=0, concat_axis=0, tiled=True)
    )
    head_grad = lax.psum_scatter(
        lax.dot_general(
            features, grad_logits, (((0,), (0,)), ((), ())), preferred_element_type=jnp.float32
        ).astype(jnp.bfloat16),
        "dp",
        scatter_dimension=0,
        tiled=True,
    ).astype(jnp.float32)
    return (summed.astype(jnp.bfloat16), head_grad, expected)


def candidate_terms(logprob, risk, seq_length):
    sent_count, cand_count = risk.shape
    scores = jnp.mean(logprob.reshape(sent_count, cand_count, seq_length), axis=2)
    raised = jnp.exp(scores)
    weights = raised / jnp.sum(raised, axis=1, keepdims=True)
    cost_value = risk.astype(jnp.float32) / 100.0
    expected = jnp.sum(weights * cost_value, axis=1)
    coeff = loss_scale * weights * (cost_value - expected[:, None]) / seq_length
    return expected, coeff


def column(row_vector, length):
    return jnp.transpose(jnp.broadcast_to(row_vector, (8, length)))[:, 0:1]


def row_stats(flags, words, totals):
    rows = totals[0].shape[0]
    widths = [t.shape[1] for t in totals]
    count = len(totals)
    col_count = widths[0]
    block_width = 2 * col_count // flags.shape[0] if flags.shape[0] else col_count

    def kernel(flags_ref, words_ref, *refs):
        logit_refs, out_ref = refs[:count], refs[count]
        peak = jnp.full((rows, 1), masked_value, jnp.float32)
        spot = column(words_ref[...], rows)
        start = 0
        pieces = []
        for ref in logit_refs:
            for b in range(ref.shape[1] // block_width):
                logits = ref[:, b * block_width : (b + 1) * block_width]
                listed = flags_ref[start // block_width] == 1
                pieces.append((ref, b, start, listed))
                top = jnp.max(logits, axis=1, keepdims=True)
                peak = jnp.where(listed, jnp.maximum(peak, top), peak)
                start += block_width
        total = jnp.zeros((rows, 1), jnp.float32)
        chosen = jnp.zeros((rows, 1), jnp.float32)
        for ref, b, begin, listed in pieces:
            logits = ref[:, b * block_width : (b + 1) * block_width]
            part = jnp.sum(jnp.exp(jnp.minimum(logits - peak, 0.0)), axis=1, keepdims=True)
            total = jnp.where(listed, total + part, total)
            lanes = lax.broadcasted_iota(jnp.int32, (rows, block_width), 1) + begin
            chosen += jnp.sum(
                jnp.where(spot == lanes.astype(jnp.float32), logits, 0.0), axis=1, keepdims=True
            )
        lane = lax.broadcasted_iota(jnp.int32, (rows, 128), 1)
        table = jnp.where(lane == 0, peak, jnp.where(lane == 1, total, chosen))
        out_ref[...] = jnp.transpose(table)[0:8, :]

    return pl.pallas_call(
        kernel,
        out_shape=jax.ShapeDtypeStruct((8, rows), jnp.float32),
        in_specs=[pl.BlockSpec(memory_space=pltpu.SMEM)]
        + [pl.BlockSpec(memory_space=pltpu.VMEM)] * (1 + count),
        out_specs=pl.BlockSpec(memory_space=pltpu.VMEM),
        compiler_params=pltpu.CompilerParams(vmem_limit_bytes=kernel_vmem),
        cost_estimate=pl.CostEstimate(
            flops=8 * rows * sum(widths),
            bytes_accessed=4 * rows * sum(widths),
            transcendentals=rows * sum(widths),
        ),
        name="row_stats",
    )(flags, words, *totals)


def row_grads(flags, words, costs, stats, totals, seq_length):
    rows = totals[0].shape[0]
    count = len(totals)
    peers = len(stats)
    cand_count = costs.shape[0]
    widths = [t.shape[1] for t in totals]
    block_width = 2 * widths[0] // flags.shape[0]
    padded = -(-cand_count // 8) * 8

    def kernel(flags_ref, words_ref, costs_ref, *refs):
        stat_refs, logit_refs = refs[:peers], refs[peers : peers + count]
        out_refs = refs[peers + count : peers + 2 * count]
        turned_refs, expected_ref = refs[peers + 2 * count : -1], refs[-1]
        peaks = [r[0:1, :] for r in stat_refs]
        peak = functools.reduce(jnp.maximum, peaks)
        total = sum(r[1:2, :] * jnp.exp(p - peak) for r, p in zip(stat_refs, peaks))
        target = sum(r[2:3, :] for r in stat_refs)
        logprob = target - peak - jnp.log(total)
        row_of = lax.broadcasted_iota(jnp.int32, (padded, rows), 1)
        first = lax.broadcasted_iota(jnp.int32, (padded, rows), 0) * seq_length
        belongs = (row_of >= first) & (row_of < first + seq_length)
        scores = jnp.sum(jnp.where(belongs, logprob, 0.0), axis=1, keepdims=True) / seq_length
        real = lax.broadcasted_iota(jnp.int32, (padded, 1), 0) < cand_count
        raised = jnp.where(real, jnp.exp(scores), 0.0)
        weights = raised / jnp.sum(raised, axis=0, keepdims=True)
        lanes = lax.broadcasted_iota(jnp.int32, (padded, 128), 1)
        subs = lax.broadcasted_iota(jnp.int32, (padded, 128), 0)
        risks = jnp.broadcast_to(costs_ref[0:1, :], (padded, 128))
        cost = jnp.sum(jnp.where(lanes == subs, risks, 0.0), axis=1, keepdims=True) / 100.0
        expected = jnp.sum(weights * cost, axis=0, keepdims=True)
        coeff = loss_scale * weights * (cost - expected) / seq_length
        row_coeff = jnp.sum(jnp.where(belongs, coeff, 0.0), axis=0, keepdims=True)
        expected_ref[...] = jnp.broadcast_to(expected, (1, 128))
        place = lax.broadcasted_iota(jnp.int32, (8, rows), 0)
        table = jnp.where(
            place == 0,
            peak,
            jnp.where(place == 1, total, jnp.where(place == 2, row_coeff, words_ref[...])),
        )
        turned = jnp.transpose(table)
        peak_col, total_col = turned[:, 0:1], turned[:, 1:2]
        coeff_col, spot = turned[:, 2:3], turned[:, 3:4]
        begin = 0
        for ref, out_ref, turned_ref in zip(logit_refs, out_refs, turned_refs):
            for b in range(ref.shape[1] // block_width):
                cols = slice(b * block_width, (b + 1) * block_width)
                listed = (flags_ref[begin // block_width] == 1).astype(jnp.float32)
                shifted = jnp.minimum(ref[:, cols] - peak_col, 0.0)
                prob = jnp.exp(shifted) / total_col * listed
                lane = lax.broadcasted_iota(jnp.int32, (rows, block_width), 1) + begin
                hit = (spot == lane.astype(jnp.float32)).astype(jnp.float32)
                value = coeff_col * (hit - prob)
                out_ref[:, cols] = value.astype(jnp.bfloat16)
                turned_ref[cols, :] = jnp.transpose(value).astype(jnp.bfloat16)
                begin += block_width

    vmem = pl.BlockSpec(memory_space=pltpu.VMEM)
    outs = pl.pallas_call(
        kernel,
        out_shape=[jax.ShapeDtypeStruct((rows, w), jnp.bfloat16) for w in widths]
        + [jax.ShapeDtypeStruct((w, rows), jnp.bfloat16) for w in widths]
        + [jax.ShapeDtypeStruct((1, 128), jnp.float32)],
        in_specs=[pl.BlockSpec(memory_space=pltpu.SMEM)] + [vmem] * (2 + peers + count),
        out_specs=[vmem] * (2 * count + 1),
        compiler_params=pltpu.CompilerParams(vmem_limit_bytes=kernel_vmem),
        cost_estimate=pl.CostEstimate(
            flops=8 * rows * sum(widths),
            bytes_accessed=6 * rows * sum(widths),
            transcendentals=rows * sum(widths),
        ),
        name="row_grads",
    )(flags, words, jnp.pad(costs.astype(jnp.float32), (0, 128 - cand_count))[None], *stats, *totals)
    return outs[:count], outs[count:-1], outs[-1]


def send_product(turned, features, order, piece):
    columns, rows = turned.shape
    count = len(order)

    def kernel(order_ref, turned_ref, in_ref, out_ref):
        left = turned_ref[...]
        for i in range(count):
            at = pl.multiple_of(order_ref[i] * piece, piece)
            value = jnp.dot(left, in_ref[:, pl.ds(at, piece)], preferred_element_type=jnp.float32)
            out_ref[:, i * piece : (i + 1) * piece] = value.astype(jnp.bfloat16)

    vmem = pl.BlockSpec(memory_space=pltpu.VMEM)
    return pl.pallas_call(
        kernel,
        out_shape=jax.ShapeDtypeStruct((columns, count * piece), jnp.bfloat16),
        in_specs=[pl.BlockSpec(memory_space=pltpu.SMEM), vmem, vmem],
        out_specs=vmem,
        compiler_params=pltpu.CompilerParams(vmem_limit_bytes=kernel_vmem),
        cost_estimate=pl.CostEstimate(
            flops=2 * rows * columns * count * piece,
            bytes_accessed=2 * (rows + columns) * count * piece,
            transcendentals=0,
        ),
        name="send_product",
    )(jnp.stack(order).astype(jnp.int32), turned, features)


def keep_product(turned, features, order, piece, received, places):
    columns, rows = turned.shape
    count = len(order)
    width = columns // 2
    middle = count // 2

    def kernel(order_ref, turned_ref, in_ref, got_ref, *out_refs):
        left = turned_ref[...]
        for i in range(count):
            at = pl.multiple_of(order_ref[i] * piece, piece)
            value = jnp.dot(left, in_ref[:, pl.ds(at, piece)], preferred_element_type=jnp.float32)
            value = value + got_ref[:, i * piece : (i + 1) * piece].astype(jnp.float32)
            for k in range(2):
                part = value[k * width : (k + 1) * width]
                at = places[k][i]
                spot = slice(at % middle * piece, (at % middle + 1) * piece)
                if at >= middle:
                    out_refs[k][:, spot] = part.astype(jnp.bfloat16)
                else:
                    out_refs[2 + k][:, spot] = part

    vmem = pl.BlockSpec(memory_space=pltpu.VMEM)
    return pl.pallas_call(
        kernel,
        out_shape=[jax.ShapeDtypeStruct((width, middle * piece), jnp.bfloat16)] * 2
        + [jax.ShapeDtypeStruct((width, middle * piece), jnp.float32)] * 2,
        in_specs=[pl.BlockSpec(memory_space=pltpu.SMEM), vmem, vmem, vmem],
        out_specs=[vmem] * 4,
        compiler_params=pltpu.CompilerParams(vmem_limit_bytes=kernel_vmem),
        cost_estimate=pl.CostEstimate(
            flops=2 * rows * columns * count * piece,
            bytes_accessed=2 * (rows + 3 * columns) * count * piece,
            transcendentals=0,
        ),
        name="keep_product",
    )(jnp.stack(order).astype(jnp.int32), turned, features, received)


def dot(left, right, dims):
    return lax.dot_general(left, right, (dims, ((), ())), preferred_element_type=jnp.float32)


def masks_of(bits):
    masks = [0]
    for bit in reversed(bits):
        masks = masks + [m | bit for m in masks]
    return masks


def halves(hidden, head, shortlist, tokens, risk):
    vocab_count = lax.axis_size("vocab")
    group = vocab_count // 2
    dp_count = lax.axis_size("dp")
    place = lax.axis_index("vocab")
    member = lax.axis_index("dp")
    half = place // group
    spot = place % group
    row_count = hidden.shape[0] // 2
    slice_width = hidden.shape[1]
    model_width, col_count = head.shape
    cand_count = risk.shape[1]
    seq_length = row_count // cand_count
    other = (place + group) % vocab_count
    bits = dp_bits()
    wide = bits[1:]
    orders = (wide, wide[::-1])
    piece_rows = model_width // dp_count
    width = col_count // 2
    cut = slice_width // 2

    first_row = member * piece_rows
    held = [
        shift_half(lax.dynamic_slice(head, (first_row, i * width), (piece_rows, width)))
        for i in range(2)
    ]
    own_rows = lax.dynamic_slice_in_dim(hidden, half * row_count, row_count, 0)
    neighbours = [shift_within(own_rows, step) for step in range(1, group)]
    far_list = shift_half(lax.dynamic_slice_in_dim(shortlist, 1 - half, 1, 0))
    far_rows = lax.dynamic_slice_in_dim(hidden, (1 - half) * row_count, row_count, 0)
    crossed = []
    for i in range(2):
        sent = after(far_rows[:, i * cut : (i + 1) * cut], held[i])
        crossed.append(shift_half(sent))
    masks = [[0], [0]]
    held = [h[None] for h in held]
    for level in range(len(wide)):
        for k in range(2):
            bit = orders[k][level]
            received = swap_dp(held[k], bit)
            held[k] = jnp.concatenate([held[k], received], axis=0)
            masks[k] = masks[k] + [m ^ bit for m in masks[k]]
    crossed = [after(c, *held) for c in crossed]
    relayed = [[shift_within(c, step) for step in range(1, group)] for c in crossed]
    far_head = jnp.zeros((model_width, col_count), jnp.bfloat16)
    for k in range(2):
        received = swap_dp(held[k], 1)
        for blocks, flip in ((held[k], 0), (received, 1)):
            for block, mask in zip(blocks, masks[k]):
                far_head = lax.dynamic_update_slice(
                    far_head, block, ((member ^ (mask | flip)) * piece_rows, k * width)
                )

    sources = [half * group + (spot - step) % group for step in range(group)]
    far_sources = [(s + group) % vocab_count for s in sources]

    def put(features, block, source, part=0):
        return lax.dynamic_update_slice(features, block, (0, source * slice_width + part * cut))

    features = jnp.zeros((row_count, model_width), jnp.bfloat16)
    for block, source in zip([own_rows] + neighbours, sources):
        features = put(features, block, source)
    for i in range(2):
        features = put(features, crossed[i], far_sources[0], i)
    for block, source in zip(relayed[0], far_sources[1:]):
        features = put(features, block, source, 0)
    for block, source in zip(relayed[1], far_sources[1:]):
        features = put(features, block, source, 1)
    totals = [dot(features, matrix, ((1,), (0,))) for matrix in (head, far_head)]

    own_list = lax.dynamic_slice_in_dim(shortlist, half, 1, 0)
    flags = jnp.concatenate([own_list[0], far_list[0]])
    words = lax.dynamic_slice_in_dim(tokens, half * row_count, row_count, 0)
    group_of = words // col_count
    within = words - group_of * col_count
    position = jnp.where(
        group_of == place, within, jnp.where(group_of == other, within + col_count, -1)
    ).astype(jnp.float32)[None]
    costs = lax.dynamic_slice_in_dim(risk, half, 1, 0)[0]
    stats = row_stats(flags, position, totals)
    gathered = [stats] + [shift_within(stats, step) for step in range(1, group)]
    (own_grad, far_grad), (own_turned, far_turned), expected_own = row_grads(
        flags, position, costs, gathered, totals, seq_length
    )

    order_masks = [masks_of(order) for order in orders]
    kept = order_masks[0]
    places = [[masks.index(m) for m in kept] for masks in order_masks]

    def core_step(turned):
        sent = send_product(turned, features, [member ^ m ^ 1 for m in kept], piece_rows)
        return swap_dp(sent, 1)

    def first_sends(turned, received):
        outs = keep_product(
            turned, features, [member ^ m for m in kept], piece_rows, received, places
        )
        return list(outs[:2]), list(outs[2:])

    def wide_steps(sends, keeps):
        for level in range(len(wide)):
            for k in range(2):
                got = swap_dp(sends[k], orders[k][level])
                total = keeps[k] + got.astype(jnp.float32)
                middle = total.shape[1] // 2
                if level + 1 < len(wide):
                    sends[k], keeps[k] = total[:, middle:].astype(jnp.bfloat16), total[:, :middle]
                else:
                    keeps[k] = total
        return jnp.concatenate(keeps, axis=0)

    far_parts = [far_turned[:width], far_turned[width:]]
    far_received = [core_step(t) for t in far_parts]
    far_first = [first_sends(t, r) for t, r in zip(far_parts, far_received)]

    share = row_count // group

    def turned_rows(value):
        pieces = [
            lax.dynamic_slice_in_dim(value, (spot + step) % group * share, share, 0)
            for step in range(1, group + 1)
        ]
        return jnp.concatenate(pieces, axis=0)

    rows_grad = (
        dot(turned_rows(own_grad), head, ((1,), (1,)))
        + dot(turned_rows(far_grad), far_head, ((1,), (1,)))
    ).astype(jnp.bfloat16)
    arrived = [
        shift_within(rows_grad[(step - 1) * share : step * share], step)
        for step in range(1, group)
    ]
    far_sums = [shift_half(wide_steps(*first).astype(jnp.bfloat16)) for first in far_first]
    own_received = core_step(own_turned)
    expected_far = shift_half(expected_own)
    first = half == 0
    expected = jnp.concatenate(
        [
            jnp.where(first, expected_own[0, :1], expected_far[0, :1]),
            jnp.where(first, expected_far[0, :1], expected_own[0, :1]),
        ]
    )
    own_sum = wide_steps(*first_sends(own_turned, own_received))
    far_sum = jnp.concatenate(far_sums, axis=0)
    head_grad = jnp.transpose(own_sum + far_sum.astype(jnp.float32))
    summed = rows_grad[(group - 1) * share :].astype(jnp.float32)
    for value in arrived:
        summed = summed + value.astype(jnp.float32)
    return (summed.astype(jnp.bfloat16), head_grad, expected)


def fits_halves(vocab_count, dp_count, hidden, head, shortlist, risk):
    return (
        vocab_count % 2 == 0
        and vocab_count >= 4
        and shortlist[0] == 2
        and dp_count & (dp_count - 1) == 0
        and dp_count == 2 * vocab_count
        and head[0] % (128 * dp_count) == 0
        and head[1] % 512 == 0
        and (head[1] // shortlist[1]) % 128 == 0
        and (head[1] // 2) % (head[1] // shortlist[1]) == 0
        and (hidden[0] // 2) % (8 * risk[1]) in range(8 * risk[1])
        and (hidden[0] // 2) % (vocab_count // 2) == 0
        and risk[1] <= 128
    )


def body(hidden, head, shortlist, tokens, risk):
    fits = fits_halves(
        lax.axis_size("vocab"),
        lax.axis_size("dp"),
        hidden.shape,
        head.shape,
        shortlist.shape,
        risk.shape,
    )
    return (halves if fits else plain)(hidden, head, shortlist, tokens, risk)


def solution(mesh):
    return jax.shard_map(
        body,
        mesh=mesh,
        in_specs=(P("dp", "vocab"), P(None, "vocab"), P("dp", "vocab"), P("dp"), P("dp", None)),
        out_specs=(P(("dp", "vocab"), None), P("dp", "vocab"), P("dp")),
        check_vma=False,
    )
```

time: 227 us -> 160 us (0.70)
  blocking collectives: 106 us -> 0 us
  starting transfers between devices: 0.08 us -> 42.1 us
  between operations: 14.1 us -> 1.31 us
  matrix products: 16.6 us -> 4.94 us
  Pallas kernels: 0 us -> 10.6 us
  local copies, waits for them, and re-layouts: 2.66 us -> 11.7 us
  waiting for transfers between devices: 80 us -> 84.7 us
  other arithmetic: 6.99 us -> 4.66 us
    all_to_all x1 -> x0, blocking collectives: 87 us -> none  [body(): lax.all_to_all(partial_value, 'vocab', split_axis=0, concat_axis=0, tiled...]
    ppermute x0 -> x34, waiting for transfers between devices: none -> 84.7 us  [the longest x8 40.7 us: shift_half(): lax.ppermute(value, 'vocab', [(i, (i + count // 2) % count) for i in rang...]
    all_gather x1 -> x0, waiting for transfers between devices: 79.3 us -> none  [body(): features = lax.all_gather(hidden, 'vocab', axis=1, tiled=True)]
    ppermute x0 -> x34, starting transfers between devices: none -> 42.1 us  [the longest x21 21 us: swap_dp(): return lax.ppermute(value, 'dp', [(i, i ^ bit) for i in range(count)])]
    dot_general x3 -> x4, matrix products: 16.6 us -> 4.94 us  [dot(): lax.dot_general(left, right, (dims, ((), ())), preferred_element_type=jnp...]
    pallas_call x0 -> x8, Pallas kernels: none -> 10.6 us  [the longest x3 4.18 us: send_product(): pl.pallas_call(kernel, out_shape=jax.ShapeDtypeStruct((columns, count * p...]
    psum x1 -> x0, blocking collectives: 9.76 us -> none  [body(): lax.psum((row_total * jnp.exp(row_peak - global_peak), chosen), 'vocab')]
    pmax x1 -> x0, blocking collectives: 8.99 us -> none  [body(): global_peak = lax.pmax(row_peak, 'vocab')]
  transfers between devices with their start and end apart: 2 -> 34, of which waited for: 1 -> 21; matrix products, arithmetic and copies ran while one was open for 4% -> 9% of each run, Pallas kernels for 0% -> 4%
where the time goes in v1:
time: 160 us
  waiting for transfers between devices  84.7 us (53%)
  starting transfers between devices  42.1 us (26%)
  local copies, waits for them, and re-layouts  11.7 us (7%)
  Pallas kernels  10.6 us (7%)
  matrix products  4.94 us (3%)
  other arithmetic  4.66 us (3%)
    ppermute x8, waiting for transfers between devices, shift_half(): lax.ppermute(value, 'vocab', [(i, (i + count // 2) % count) for i in rang...  40.7 us
    ppermute x21, waiting for transfers between devices, swap_dp(): return lax.ppermute(value, 'dp', [(i, i ^ bit) for i in range(count)])  31.7 us
    ppermute x21, starting transfers between devices, swap_dp(): return lax.ppermute(value, 'dp', [(i, i ^ bit) for i in range(count)])  21 us
    ppermute x8, starting transfers between devices, shift_half(): lax.ppermute(value, 'vocab', [(i, (i + count // 2) % count) for i in rang...  16.3 us
    ppermute x5, waiting for transfers between devices, shift_within(): return lax.ppermute(value, 'vocab', pairs)  12.3 us
    dot_general x4, matrix products, dot(): lax.dot_general(left, right, (dims, ((), ())), preferred_element_type=jnp...  4.94 us
    ppermute x5, starting transfers between devices, shift_within(): return lax.ppermute(value, 'vocab', pairs)  4.75 us
    pallas_call x3, Pallas kernels, send_product(): pl.pallas_call(kernel, out_shape=jax.ShapeDtypeStruct((columns, count * p...  4.18 us
  transfers between devices with their start and end apart: 34, of which 21 were waited for; matrix products, arithmetic and copies ran while one was open for 9% of the time, Pallas kernels for 4%

profile of v1, /device:TPU:0, one launch (start us, length us, event | category | flops | bytes accessed | tf_op | source)
XLA Modules:
  0.0 160.0 jit_solution(2102174383611074817)
XLA Ops:
  0.7 2.0 %constant_dynamic-slice_fusion.10 = (bf16[512,256]{1,0:T(8,128)(2,1)}, bf16[512,256]{1,0:T(8,128)(2,1)}) fusion(bf16[4096,512]{1,0:T(8,128)(2,1)} %param.6, s32[]{:T(128)S(6)} %select_n.155), kind=kLoop, calls=%fused_computation.84 | loop fusion | bytes 1048580 | tf_op jit(solution)/shard_map/dynamic_slice | solution.py:345
  2.6 4.1 %collective-permute-start.2 = (bf16[512,256]{1,0:T(8,128)(2,1)}, bf16[512,256]{1,0:T(8,128)(2,1)S(1)}, u32[]{:S(2)}, u32[]{:S(2)}) collective-permute-start(bf16[512,256]{1,0:T(8,128)(2,1)} %get-tuple-element.51), channel_id=1, source_target_pairs={{0,2},{1,3},{2,0},{3,1},{4,6},{5,7},{6,4},{7,5},{8,10},{9,11},{10,... | collective-permute-start | bytes 786440 | tf_op jit(solution)/shard_map/ppermute | solution.py:27
  10.8 2.7 %collective-permute-start = (s32[1,2]{1,0:T(1,128)S(1)}, s32[1,2]{1,0:T(1,128)S(1)}, u32[]{:S(2)}, u32[]{:S(2)}) collective-permute-start(s32[1,2]{1,0:T(1,128)S(1)} %get-tuple-element.61), channel_id=1, source_target_pairs={{0,2},{1,3},{2,0},{3,1},{4,6},{5,7},{6,4},{7,5},{8,10},{9,11},{10,... | collective-permute-start | bytes 32 | tf_op jit(solution)/shard_map/ppermute | solution.py:27
  14.4 11.0 %collective-permute-done.2 = bf16[512,256]{1,0:T(8,128)(2,1)S(1)} collective-permute-done((bf16[512,256]{1,0:T(8,128)(2,1)}, bf16[512,256]{1,0:T(8,128)(2,1)S(1)}, u32[]{:S(2)}, u32[]{:S(2)}) %collective-permute-start.2) | collective-permute-done | bytes 262176 | tf_op jit(solution)/shard_map/ppermute | solution.py:27
  27.2 3.0 %collective-permute-done.6 = bf16[512,256]{1,0:T(8,128)(2,1)S(1)} collective-permute-done((bf16[512,256]{1,0:T(8,128)(2,1)}, bf16[512,256]{1,0:T(8,128)(2,1)S(1)}, u32[]{:S(2)}, u32[]{:S(2)}) %collective-permute-start.6) | collective-permute-done | bytes 262176 | tf_op jit(solution)/shard_map/ppermute | solution.py:27
  32.1 2.6 %collective-permute-start.9 = (bf16[240,512]{1,0:T(8,128)(2,1)}, bf16[240,512]{1,0:T(8,128)(2,1)S(1)}, u32[]{:S(2)}, u32[]{:S(2)}) collective-permute-start(bf16[240,512]{1,0:T(8,128)(2,1)} %get-tuple-element.26), channel_id=1, source_target_pairs={{0,2},{1,3},{2,0},{3,1},{4,6},{5,7},{6,4},{7,5},{8,10},{9,11},{10,... | collective-permute-start | bytes 737288 | tf_op jit(solution)/shard_map/ppermute | solution.py:27
  35.3 4.0 %collective-permute-done.7 = bf16[1,512,256]{2,1,0:T(8,128)(2,1)S(1)} collective-permute-done((bf16[1,512,256]{2,1,0:T(8,128)(2,1)S(1)}, bf16[1,512,256]{2,1,0:T(8,128)(2,1)S(1)}, u32[]{:S(2)}, u32[]{:S(2)}) %collective-permute-start.7) | collective-permute-done | bytes 262176 | tf_op jit(solution)/shard_map/ppermute | solution.py:22
  42.4 6.4 %collective-permute-done.5 = bf16[2,512,256]{2,1,0:T(8,128)(2,1)S(1)} collective-permute-done((bf16[2,512,256]{2,1,0:T(8,128)(2,1)S(1)}, bf16[2,512,256]{2,1,0:T(8,128)(2,1)S(1)}, u32[]{:S(2)}, u32[]{:S(2)}) %collective-permute-start.5) | collective-permute-done | bytes 524320 | tf_op jit(solution)/shard_map/ppermute | solution.py:22
  52.0 3.3 %collective-permute-done.9 = bf16[240,512]{1,0:T(8,128)(2,1)S(1)} collective-permute-done((bf16[240,512]{1,0:T(8,128)(2,1)}, bf16[240,512]{1,0:T(8,128)(2,1)S(1)}, u32[]{:S(2)}, u32[]{:S(2)}) %collective-permute-start.9) | collective-permute-done | bytes 245792 | tf_op jit(solution)/shard_map/ppermute | solution.py:27
  55.3 2.0 %collective-permute-start.11 = (bf16[240,512]{1,0:T(8,128)(2,1)S(1)}, bf16[240,512]{1,0:T(8,128)(2,1)S(1)}, u32[]{:S(2)}, u32[]{:S(2)}) collective-permute-start(bf16[240,512]{1,0:T(8,128)(2,1)S(1)} %collective-permute-done.9), channel_id=1, source_target_pairs={{0,1},{1,0},{2,3},{3,2},{4,5},{5,4},{6,7},{7,6},{8,9},{9,8},{10,11... | collective-permute-start | bytes 737288 | tf_op jit(solution)/shard_map/ppermute | solution.py:34
  57.4 6.5 %collective-permute-done.10 = bf16[240,512]{1,0:T(8,128)(2,1)S(1)} collective-permute-done((bf16[240,512]{1,0:T(8,128)(2,1)S(1)}, bf16[240,512]{1,0:T(8,128)(2,1)S(1)}, u32[]{:S(2)}, u32[]{:S(2)}) %collective-permute-start.10) | collective-permute-done | bytes 245792 | tf_op jit(solution)/shard_map/ppermute | solution.py:34
  63.9 2.6 %collective-permute-done.11 = bf16[240,512]{1,0:T(8,128)(2,1)S(1)} collective-permute-done((bf16[240,512]{1,0:T(8,128)(2,1)S(1)}, bf16[240,512]{1,0:T(8,128)(2,1)S(1)}, u32[]{:S(2)}, u32[]{:S(2)}) %collective-permute-start.11) | collective-permute-done | bytes 245792 | tf_op jit(solution)/shard_map/ppermute | solution.py:34
  71.1 3.2 %collective-permute-done.14.refs_1_ = f32[8,240]{1,0:T(8,128)S(1)} collective-permute-done((f32[8,240]{1,0:T(8,128)S(1)}, f32[8,240]{1,0:T(8,128)S(1)}, u32[]{:S(2)}, u32[]{:S(2)}) %collective-permute-start.14) | collective-permute-done | bytes 7712 | tf_op jit(solution)/shard_map/ppermute | solution.py:34
  83.9 3.3 %collective-permute-start.33 = (f32[1,128]{1,0:T(1,128)S(1)}, f32[1,128]{1,0:T(1,128)S(1)}, u32[]{:S(2)}, u32[]{:S(2)}) collective-permute-start(f32[1,128]{1,0:T(1,128)S(1)} %get-tuple-element.44), channel_id=1, source_target_pairs={{0,2},{1,3},{2,0},{3,1},{4,6},{5,7},{6,4},{7,5},{8,10},{9,11},{10,... | collective-permute-start | bytes 1544 | tf_op jit(solution)/shard_map/ppermute | solution.py:27
  90.1 15.8 %collective-permute-done.33 = f32[1,128]{1,0:T(1,128)S(1)} collective-permute-done((f32[1,128]{1,0:T(1,128)S(1)}, f32[1,128]{1,0:T(1,128)S(1)}, u32[]{:S(2)}, u32[]{:S(2)}) %collective-permute-start.33) | collective-permute-done | bytes 544 | tf_op jit(solution)/shard_map/ppermute | solution.py:27
  109.8 2.4 %add_convert_fusion = bf16[120,4096]{1,0:T(8,128)(2,1)} fusion(bf16[120,4096]{1,0:T(8,128)(2,1)} %collective-permute-done.15, bf16[240,4096]{1,0:T(8,128)(2,1)S(1)} %copy-done.3), kind=kLoop, calls=%fused_computation.2 | loop fusion | flops 1966080 | bytes 2949120 | tf_op jit(solution)/shard_map/convert_element_type | solution.py:470
  116.2 2.3 %collective-permute-start.23 = (bf16[128,512]{1,0:T(8,128)(2,1)S(1)}, bf16[128,512]{1,0:T(8,128)(2,1)S(1)}, u32[]{:S(2)}, u32[]{:S(2)}) collective-permute-start(bf16[128,512]{1,0:T(8,128)(2,1)S(1)} %slice.128), channel_id=1, source_target_pairs={{0,16},{4,20},{8,24},{12,28},{16,0},{20,4},{24,8},{28,12},{1,17},{... | collective-permute-start | bytes 393224 | tf_op jit(solution)/shard_map/ppermute | solution.py:22
  118.5 2.8 %collective-permute-done.24 = bf16[128,1024]{1,0:T(8,128)(2,1)S(1)} collective-permute-done((bf16[128,1024]{1,0:T(8,128)(2,1)S(1)}, bf16[128,1024]{1,0:T(8,128)(2,1)S(1)}, u32[]{:S(2)}, u32[]{:S(2)}) %collective-permute-start.24) | collective-permute-done | bytes 262176 | tf_op jit(solution)/shard_map/ppermute | solution.py:22
  124.2 2.8 %collective-permute-done.30 = bf16[128,1024]{1,0:T(8,128)(2,1)S(1)} collective-permute-done((bf16[128,1024]{1,0:T(8,128)(2,1)S(1)}, bf16[128,1024]{1,0:T(8,128)(2,1)S(1)}, u32[]{:S(2)}, u32[]{:S(2)}) %collective-permute-start.30) | collective-permute-done | bytes 262176 | tf_op jit(solution)/shard_map/ppermute | solution.py:22
  131.5 3.1 %collective-permute-start.26 = (bf16[256,512]{1,0:T(8,128)(2,1)S(1)}, bf16[256,512]{1,0:T(8,128)(2,1)S(1)}, u32[]{:S(2)}, u32[]{:S(2)}) collective-permute-start(bf16[256,512]{1,0:T(8,128)(2,1)S(1)} %pad_maximum_fusion.4), channel_id=1, source_target_pairs={{0,2},{1,3},{2,0},{3,1},{4,6},{5,7},{6,4},{7,5},{8,10},{9,11},{10,... | collective-permute-start | bytes 786440 | tf_op jit(solution)/shard_map/ppermute | solution.py:27
  136.2 7.0 %collective-permute-done.17 = bf16[256,1024]{1,0:T(8,128)(2,1)S(1)} collective-permute-done((bf16[256,1024]{1,0:T(8,128)(2,1)S(1)}, bf16[256,1024]{1,0:T(8,128)(2,1)S(1)}, u32[]{:S(2)}, u32[]{:S(2)}) %collective-permute-start.17) | collective-permute-done | bytes 524320 | tf_op jit(solution)/shard_map/ppermute | solution.py:22
  146.0 2.4 %collective-permute-start.20 = (bf16[256,512]{1,0:T(8,128)(2,1)S(1)}, bf16[256,512]{1,0:T(8,128)(2,1)S(1)}, u32[]{:S(2)}, u32[]{:S(2)}) collective-permute-start(bf16[256,512]{1,0:T(8,128)(2,1)S(1)} %slice.123), channel_id=1, source_target_pairs={{0,8},{4,12},{8,0},{12,4},{16,24},{20,28},{24,16},{28,20},{1,9},{5... | collective-permute-start | bytes 786440 | tf_op jit(solution)/shard_map/ppermute | solution.py:22
  150.5 2.3 %collective-permute-done.20 = bf16[256,512]{1,0:T(8,128)(2,1)S(1)} collective-permute-done((bf16[256,512]{1,0:T(8,128)(2,1)S(1)}, bf16[256,512]{1,0:T(8,128)(2,1)S(1)}, u32[]{:S(2)}, u32[]{:S(2)}) %collective-permute-start.20) | collective-permute-done | bytes 262176 | tf_op jit(solution)/shard_map/ppermute | solution.py:22
  152.8 5.7 %collective-permute-done.32 = bf16[256,512]{1,0:T(8,128)(2,1)S(1)} collective-permute-done((bf16[256,512]{1,0:T(8,128)(2,1)S(1)}, bf16[256,512]{1,0:T(8,128)(2,1)S(1)}, u32[]{:S(2)}, u32[]{:S(2)}) %collective-permute-start.32) | collective-permute-done | bytes 262176 | tf_op jit(solution)/shard_map/ppermute | solution.py:27
  (140 shorter events, 55.6 us)
Async XLA Ops:
  2.6 22.8 %collective-permute-start.2 = (bf16[512,256]{1,0:T(8,128)(2,1)}, bf16[512,256]{1,0:T(8,128)(2,1)S(1)}, u32[]{:S(2)}, u32[]{:S(2)}) collective-permute-start(bf16[512,256]{1,0:T(8,128)(2,1)} %get-tuple-element.51), channel_id=1, source_target_pairs={{0,2},{1,3},{2,0},{3,1},{4,6},{5,7},{6,4},{7,5},{8,10},{9,11},{10,... | collective-permute-start | bytes 786440 | tf_op jit(solution)/shard_map/ppermute | solution.py:27
  6.7 23.5 %collective-permute-start.6 = (bf16[512,256]{1,0:T(8,128)(2,1)}, bf16[512,256]{1,0:T(8,128)(2,1)S(1)}, u32[]{:S(2)}, u32[]{:S(2)}) collective-permute-start(bf16[512,256]{1,0:T(8,128)(2,1)} %get-tuple-element.50), channel_id=1, source_target_pairs={{0,2},{1,3},{2,0},{3,1},{4,6},{5,7},{6,4},{7,5},{8,10},{9,11},{10,... | collective-permute-start | bytes 786440 | tf_op jit(solution)/shard_map/ppermute | solution.py:27
  8.9 32.2 %collective-permute-start.1 = (bf16[240,1024]{1,0:T(8,128)(2,1)}, bf16[240,1024]{1,0:T(8,128)(2,1)}, u32[]{:S(2)}, u32[]{:S(2)}) collective-permute-start(bf16[240,1024]{1,0:T(8,128)(2,1)} %get-tuple-element.49), channel_id=1, source_target_pairs={{0,1},{1,0},{2,3},{3,2},{4,5},{5,4},{6,7},{7,6},{8,9},{9,8},{10,11... | collective-permute-start | bytes 1474568 | tf_op jit(solution)/shard_map/ppermute | solution.py:34
  10.8 21.0 %collective-permute-start = (s32[1,2]{1,0:T(1,128)S(1)}, s32[1,2]{1,0:T(1,128)S(1)}, u32[]{:S(2)}, u32[]{:S(2)}) collective-permute-start(s32[1,2]{1,0:T(1,128)S(1)} %get-tuple-element.61), channel_id=1, source_target_pairs={{0,2},{1,3},{2,0},{3,1},{4,6},{5,7},{6,4},{7,5},{8,10},{9,11},{10,... | collective-permute-start | bytes 32 | tf_op jit(solution)/shard_map/ppermute | solution.py:27
  25.4 9.4 %collective-permute-start.4 = (bf16[1,512,256]{2,1,0:T(8,128)(2,1)S(1)}, bf16[1,512,256]{2,1,0:T(8,128)(2,1)S(1)}, u32[]{:S(2)}, u32[]{:S(2)}) collective-permute-start(bf16[1,512,256]{2,1,0:T(8,128)(2,1)S(1)} %bitcast.90), channel_id=1, source_target_pairs={{0,8},{4,12},{8,0},{12,4},{16,24},{20,28},{24,16},{28,20},{1,9},{5... | collective-permute-start | bytes 786440 | tf_op jit(solution)/shard_map/ppermute | solution.py:22
  31.8 20.1 %collective-permute-start.3 = (bf16[240,512]{1,0:T(8,128)(2,1)}, bf16[240,512]{1,0:T(8,128)(2,1)S(1)}, u32[]{:S(2)}, u32[]{:S(2)}) collective-permute-start(bf16[240,512]{1,0:T(8,128)(2,1)} %get-tuple-element.24), channel_id=1, source_target_pairs={{0,2},{1,3},{2,0},{3,1},{4,6},{5,7},{6,4},{7,5},{8,10},{9,11},{10,... | collective-permute-start | bytes 737288 | tf_op jit(solution)/shard_map/ppermute | solution.py:27
  32.1 23.1 %collective-permute-start.9 = (bf16[240,512]{1,0:T(8,128)(2,1)}, bf16[240,512]{1,0:T(8,128)(2,1)S(1)}, u32[]{:S(2)}, u32[]{:S(2)}) collective-permute-start(bf16[240,512]{1,0:T(8,128)(2,1)} %get-tuple-element.26), channel_id=1, source_target_pairs={{0,2},{1,3},{2,0},{3,1},{4,6},{5,7},{6,4},{7,5},{8,10},{9,11},{10,... | collective-permute-start | bytes 737288 | tf_op jit(solution)/shard_map/ppermute | solution.py:27
  34.8 14.0 %collective-permute-start.5 = (bf16[2,512,256]{2,1,0:T(8,128)(2,1)S(1)}, bf16[2,512,256]{2,1,0:T(8,128)(2,1)S(1)}, u32[]{:S(2)}, u32[]{:S(2)}) collective-permute-start(bf16[2,512,256]{2,1,0:T(8,128)(2,1)S(1)} %pad_maximum_fusion.2), channel_id=1, source_target_pairs={{0,16},{4,20},{8,24},{12,28},{16,0},{20,4},{24,8},{28,12},{1,17},{... | collective-permute-start | bytes 1572872 | tf_op jit(solution)/shard_map/ppermute | solution.py:22
  39.4 10.5 %collective-permute-start.8 = (bf16[2,512,256]{2,1,0:T(8,128)(2,1)S(1)}, bf16[2,512,256]{2,1,0:T(8,128)(2,1)S(1)}, u32[]{:S(2)}, u32[]{:S(2)}) collective-permute-start(bf16[2,512,256]{2,1,0:T(8,128)(2,1)S(1)} %pad_maximum_fusion.3), channel_id=1, source_target_pairs={{0,8},{4,12},{8,0},{12,4},{16,24},{20,28},{24,16},{28,20},{1,9},{5... | collective-permute-start | bytes 1572872 | tf_op jit(solution)/shard_map/ppermute | solution.py:22
  48.9 18.9 %collective-permute-start.12 = (bf16[4,512,256]{2,1,0:T(8,128)(2,1)S(1)}, bf16[4,512,256]{2,1,0:T(8,128)(2,1)S(1)}, u32[]{:S(2)}, u32[]{:S(2)}) collective-permute-start(bf16[4,512,256]{2,1,0:T(8,128)(2,1)S(1)} %pad_maximum_fusion), channel_id=1, source_target_pairs={{0,4},{4,0},{8,12},{12,8},{16,20},{20,16},{24,28},{28,24},{1,5},{5... | collective-permute-start | bytes 3145736 | tf_op jit(solution)/shard_map/ppermute | solution.py:22
  50.0 18.1 %collective-permute-start.13 = (bf16[4,512,256]{2,1,0:T(8,128)(2,1)S(1)}, bf16[4,512,256]{2,1,0:T(8,128)(2,1)S(1)}, u32[]{:S(2)}, u32[]{:S(2)}) collective-permute-start(bf16[4,512,256]{2,1,0:T(8,128)(2,1)S(1)} %pad_maximum_fusion.1), channel_id=1, source_target_pairs={{0,4},{4,0},{8,12},{12,8},{16,20},{20,16},{24,28},{28,24},{1,5},{5... | collective-permute-start | bytes 3145736 | tf_op jit(solution)/shard_map/ppermute | solution.py:22
  55.3 11.3 %collective-permute-start.11 = (bf16[240,512]{1,0:T(8,128)(2,1)S(1)}, bf16[240,512]{1,0:T(8,128)(2,1)S(1)}, u32[]{:S(2)}, u32[]{:S(2)}) collective-permute-start(bf16[240,512]{1,0:T(8,128)(2,1)S(1)} %collective-permute-done.9), channel_id=1, source_target_pairs={{0,1},{1,0},{2,3},{3,2},{4,5},{5,4},{6,7},{7,6},{8,9},{9,8},{10,11... | collective-permute-start | bytes 737288 | tf_op jit(solution)/shard_map/ppermute | solution.py:34
  77.6 28.9 %collective-permute-start.21 = (bf16[256,2048]{1,0:T(8,128)(2,1)}, bf16[256,2048]{1,0:T(8,128)(2,1)}, u32[]{:S(2)}, u32[]{:S(2)}) collective-permute-start(bf16[256,2048]{1,0:T(8,128)(2,1)} %send_product.4), channel_id=1, source_target_pairs={{0,4},{4,0},{8,12},{12,8},{16,20},{20,16},{24,28},{28,24},{1,5},{5... | collective-permute-start | bytes 3145736 | tf_op jit(solution)/shard_map/ppermute | solution.py:22
  83.4 26.3 %collective-permute-start.15 = (bf16[120,4096]{1,0:T(8,128)(2,1)}, bf16[120,4096]{1,0:T(8,128)(2,1)}, u32[]{:S(2)}, u32[]{:S(2)}) collective-permute-start(bf16[120,4096]{1,0:T(8,128)(2,1)} %slice.89), channel_id=1, source_target_pairs={{0,1},{1,0},{2,3},{3,2},{4,5},{5,4},{6,7},{7,6},{8,9},{9,8},{10,11... | collective-permute-start | bytes 2949128 | tf_op jit(solution)/shard_map/ppermute | solution.py:34
  83.9 21.9 %collective-permute-start.33 = (f32[1,128]{1,0:T(1,128)S(1)}, f32[1,128]{1,0:T(1,128)S(1)}, u32[]{:S(2)}, u32[]{:S(2)}) collective-permute-start(f32[1,128]{1,0:T(1,128)S(1)} %get-tuple-element.44), channel_id=1, source_target_pairs={{0,2},{1,3},{2,0},{3,1},{4,6},{5,7},{6,4},{7,5},{8,10},{9,11},{10,... | collective-permute-start | bytes 1544 | tf_op jit(solution)/shard_map/ppermute | solution.py:27
  88.2 25.5 %collective-permute-start.27 = (bf16[256,2048]{1,0:T(8,128)(2,1)S(1)}, bf16[256,2048]{1,0:T(8,128)(2,1)S(1)}, u32[]{:S(2)}, u32[]{:S(2)}) collective-permute-start(bf16[256,2048]{1,0:T(8,128)(2,1)S(1)} %send_product.5), channel_id=1, source_target_pairs={{0,4},{4,0},{8,12},{12,8},{16,20},{20,16},{24,28},{28,24},{1,5},{5... | collective-permute-start | bytes 3145736 | tf_op jit(solution)/shard_map/ppermute | solution.py:22
  89.5 40.1 %collective-permute-start.16 = (bf16[512,2048]{1,0:T(8,128)(2,1)S(1)}, bf16[512,2048]{1,0:T(8,128)(2,1)S(1)}, u32[]{:S(2)}, u32[]{:S(2)}) collective-permute-start(bf16[512,2048]{1,0:T(8,128)(2,1)S(1)} %send_product.3), channel_id=1, source_target_pairs={{0,4},{4,0},{8,12},{12,8},{16,20},{20,16},{24,28},{28,24},{1,5},{5... | collective-permute-start | bytes 6291464 | tf_op jit(solution)/shard_map/ppermute | solution.py:22
  115.3 11.7 %collective-permute-start.30 = (bf16[128,1024]{1,0:T(8,128)(2,1)S(1)}, bf16[128,1024]{1,0:T(8,128)(2,1)S(1)}, u32[]{:S(2)}, u32[]{:S(2)}) collective-permute-start(bf16[128,1024]{1,0:T(8,128)(2,1)S(1)} %get-tuple-element.43), channel_id=1, source_target_pairs={{0,16},{4,20},{8,24},{12,28},{16,0},{20,4},{24,8},{28,12},{1,17},{... | collective-permute-start | bytes 786440 | tf_op jit(solution)/shard_map/ppermute | solution.py:22
  116.2 13.3 %collective-permute-start.23 = (bf16[128,512]{1,0:T(8,128)(2,1)S(1)}, bf16[128,512]{1,0:T(8,128)(2,1)S(1)}, u32[]{:S(2)}, u32[]{:S(2)}) collective-permute-start(bf16[128,512]{1,0:T(8,128)(2,1)S(1)} %slice.128), channel_id=1, source_target_pairs={{0,16},{4,20},{8,24},{12,28},{16,0},{20,4},{24,8},{28,12},{1,17},{... | collective-permute-start | bytes 393224 | tf_op jit(solution)/shard_map/ppermute | solution.py:22
  123.2 11.4 %collective-permute-start.29 = (bf16[128,512]{1,0:T(8,128)(2,1)S(1)}, bf16[128,512]{1,0:T(8,128)(2,1)S(1)}, u32[]{:S(2)}, u32[]{:S(2)}) collective-permute-start(bf16[128,512]{1,0:T(8,128)(2,1)S(1)} %slice.126), channel_id=1, source_target_pairs={{0,16},{4,20},{8,24},{12,28},{16,0},{20,4},{24,8},{28,12},{1,17},{... | collective-permute-start | bytes 393224 | tf_op jit(solution)/shard_map/ppermute | solution.py:22
  130.9 12.4 %collective-permute-start.17 = (bf16[256,1024]{1,0:T(8,128)(2,1)S(1)}, bf16[256,1024]{1,0:T(8,128)(2,1)S(1)}, u32[]{:S(2)}, u32[]{:S(2)}) collective-permute-start(bf16[256,1024]{1,0:T(8,128)(2,1)S(1)} %get-tuple-element.32), channel_id=1, source_target_pairs={{0,8},{4,12},{8,0},{12,4},{16,24},{20,28},{24,16},{28,20},{1,9},{5... | collective-permute-start | bytes 1572872 | tf_op jit(solution)/shard_map/ppermute | solution.py:22
  131.5 21.3 %collective-permute-start.26 = (bf16[256,512]{1,0:T(8,128)(2,1)S(1)}, bf16[256,512]{1,0:T(8,128)(2,1)S(1)}, u32[]{:S(2)}, u32[]{:S(2)}) collective-permute-start(bf16[256,512]{1,0:T(8,128)(2,1)S(1)} %pad_maximum_fusion.4), channel_id=1, source_target_pairs={{0,2},{1,3},{2,0},{3,1},{4,6},{5,7},{6,4},{7,5},{8,10},{9,11},{10,... | collective-permute-start | bytes 786440 | tf_op jit(solution)/shard_map/ppermute | solution.py:27
  134.6 11.1 %collective-permute-start.19 = (bf16[256,1024]{1,0:T(8,128)(2,1)S(1)}, bf16[256,1024]{1,0:T(8,128)(2,1)S(1)}, u32[]{:S(2)}, u32[]{:S(2)}) collective-permute-start(bf16[256,1024]{1,0:T(8,128)(2,1)S(1)} %get-tuple-element.34), channel_id=1, source_target_pairs={{0,16},{4,20},{8,24},{12,28},{16,0},{20,4},{24,8},{28,12},{1,17},{... | collective-permute-start | bytes 1572872 | tf_op jit(solution)/shard_map/ppermute | solution.py:22
  148.4 10.1 %collective-permute-start.32 = (bf16[256,512]{1,0:T(8,128)(2,1)S(1)}, bf16[256,512]{1,0:T(8,128)(2,1)S(1)}, u32[]{:S(2)}, u32[]{:S(2)}) collective-permute-start(bf16[256,512]{1,0:T(8,128)(2,1)S(1)} %pad_maximum_fusion.5), channel_id=1, source_target_pairs={{0,2},{1,3},{2,0},{3,1},{4,6},{5,7},{6,4},{7,5},{8,10},{9,11},{10,... | collective-permute-start | bytes 786440 | tf_op jit(solution)/shard_map/ppermute | solution.py:27
  (20 other events, 200.2 us)
